TPU v7x, 128 devices: a whole 4x4x4 slice. The times are simulated.
128 devices in a mesh: side: 2 (over y_hi), dev: 64 (over y_lo, z, x, core).
Axes of the slice: x: 4, y: 4 (y_hi: 2, y_lo: 2; y = y_hi * 2 + y_lo), z: 4, core: 2. Of those that a mesh axis runs over, the one named last changes fastest.
Arguments:
- queries: bfloat16 [2048, 8192], P('dev', 'side'), may hold values from -6 to 6
- cache_keys: bfloat16 [2048, 256, 512], P('dev', None, 'side'), may hold values from -6 to 6
- cache_values: bfloat16 [2048, 256, 512], P('dev', None, 'side'), may hold values from -6 to 6
- new_key: bfloat16 [2048, 512], P('dev', 'side'), may hold values from -15 to 15
- new_value: bfloat16 [2048, 512], P('dev', 'side'), may hold values from -6 to 6
- cache_lengths: int32 [2048], P('dev'), may hold values from 2 to 256, as said below
- hidden: bfloat16 [2048, 4096], P('dev'), may hold values from -6 to 6
- norm_gain: bfloat16 [4096], replicated, may hold values from 0.099609375 to 1.8984375
- expert_ids: int32 [2048, 8], P('dev'), may hold values from 0 to 63, all different within a row; in each aligned block of 32 rows (0 to 31, 32 to 63, ...) at most 8 rows name the same one
- router_probs: float32 [2048, 8], P('dev'), may hold values from 0.02 to 1
- w_gate: bfloat16 [64, 4096, 1536], P('dev', None, 'side'), may hold values from -0.09375 to 0.09375
- w_up: bfloat16 [64, 4096, 1536], P('dev', None, 'side'), may hold values from -0.09375 to 0.09375
- w_down: bfloat16 [64, 1536, 4096], P('dev', 'side'), may hold values from -0.15625 to 0.15625
Outputs:
- context: bfloat16 [2048, 8192], P('dev', 'side')
- moe_out: bfloat16 [2048, 4096], P('dev')
Inputs may be any that keep to these rules, and one draw needn't show every extreme that they name: `expert_ids`: in each aligned block of 32 rows (the rows of one dev index) no expert is named more than 8 times, a bound that some block reaches. `cache_lengths`: every aligned block of 32 tokens holds a token with 256 valid positions.
All inputs are finite; a program needn't handle non-finite values.
Results may differ from a plain program's by a relative error of at most 0.012.
Values may be sent and summed in bfloat16 or wider, within the bound.
A program may use at most 128 MiB of HBM per device.

v0:
```python
import jax
import jax.numpy as jnp
from jax import lax
from jax.sharding import PartitionSpec as P

HEADS = 64
KV_HEADS = 4
HEAD_DIM = 128


def route_onehot(block_ids, expert_count, capacity):
    flat_ids = block_ids.reshape(-1)
    expert_hot = (flat_ids[:, None] == jnp.arange(expert_count, dtype=jnp.int32)[None, :]).astype(
        jnp.int32
    )
    earlier = jnp.cumsum(expert_hot, axis=0) - expert_hot
    slot_rank = jnp.sum(earlier * expert_hot, axis=1)
    slot_hot = (slot_rank[:, None] == jnp.arange(capacity, dtype=jnp.int32)[None, :]).astype(
        jnp.float32
    )
    route_hot = expert_hot.astype(jnp.float32)[:, :, None] * slot_hot[:, None, :]
    return route_hot.reshape(block_ids.shape[0], block_ids.shape[1], expert_count, capacity)


def attend_local(queries, cache_keys, cache_values, new_key, new_value, cache_lengths):
    row_count = queries.shape[0]
    cache_len = cache_keys.shape[1]
    groups = cache_keys.shape[2] // HEAD_DIM
    per_group = HEADS // KV_HEADS
    score_scale = HEAD_DIM ** (-0.5)
    query_heads = queries.reshape(row_count, groups, per_group, HEAD_DIM)
    key_heads = cache_keys.reshape(row_count, cache_len, groups, HEAD_DIM)
    value_heads = cache_values.reshape(row_count, cache_len, groups, HEAD_DIM)
    scores = (
        jnp.einsum("tgqd,tlgd->tgql", query_heads, key_heads, preferred_element_type=jnp.float32)
        * score_scale
    )
    own_key = new_key.reshape(row_count, groups, HEAD_DIM)
    own_score = (
        jnp.einsum("tgqd,tgd->tgq", query_heads, own_key, preferred_element_type=jnp.float32)
        * score_scale
    )
    visible = jnp.arange(cache_len, dtype=jnp.int32)[None, :] < cache_lengths[:, None]
    scores = jnp.where(visible[:, None, None, :], scores, -1e30)
    top_score = jnp.maximum(jnp.max(scores, axis=3), own_score)
    exp_scores = jnp.exp(scores - top_score[..., None])
    own_exp = jnp.exp(own_score - top_score)
    denominator = jnp.sum(exp_scores, axis=3) + own_exp
    attn_weights = (exp_scores / denominator[..., None]).astype(jnp.bfloat16)
    own_prob = (own_exp / denominator).astype(jnp.bfloat16)
    combined = jnp.einsum(
        "tgql,tlgd->tgqd", attn_weights, value_heads, preferred_element_type=jnp.float32
    )
    own_value = new_value.reshape(row_count, groups, 1, HEAD_DIM).astype(jnp.float32)
    combined = combined + own_prob.astype(jnp.float32)[..., None] * own_value
    return combined.reshape(row_count, groups * per_group * HEAD_DIM).astype(jnp.bfloat16)


def per_device(
    queries,
    cache_keys,
    cache_values,
    new_key,
    new_value,
    cache_lengths,
    hidden,
    norm_gain,
    expert_ids,
    router_probs,
    w_gate,
    w_up,
    w_down,
):
    context = attend_local(queries, cache_keys, cache_values, new_key, new_value, cache_lengths)
    row_count = hidden.shape[0]
    top_count = expert_ids.shape[1]
    devices = lax.axis_size("dev")
    experts = w_gate.shape[0] * devices
    capacity = max(2, 2 * row_count * top_count // experts)
    gate_share = router_probs / jnp.sum(router_probs, axis=1, keepdims=True)
    hidden_wide = hidden.astype(jnp.float32)
    inverse = lax.rsqrt(jnp.mean(hidden_wide * hidden_wide, axis=1, keepdims=True) + 1e-06)
    normed = (hidden_wide * inverse * norm_gain.astype(jnp.float32)[None, :]).astype(jnp.bfloat16)
    route_hot = route_onehot(expert_ids, experts, capacity)
    slot_hot = jnp.sum(route_hot, axis=1)
    slot_gate = jnp.sum(route_hot * gate_share[:, :, None, None], axis=1)
    buffer = jnp.einsum(
        "rec,rd->ecd", slot_hot.astype(jnp.bfloat16), normed, preferred_element_type=jnp.float32
    ).astype(jnp.bfloat16)
    row_block = lax.all_to_all(buffer, "dev", split_axis=0, concat_axis=0, tiled=True)
    gate_act = jnp.einsum("scd,df->scf", row_block, w_gate[0], preferred_element_type=jnp.float32)
    up_act = jnp.einsum("scd,df->scf", row_block, w_up[0], preferred_element_type=jnp.float32)
    activation = (jax.nn.silu(gate_act) * up_act).astype(jnp.bfloat16)
    partial_out = jnp.einsum(
        "scf,fd->scd", activation, w_down[0], preferred_element_type=jnp.float32
    ).astype(jnp.bfloat16)
    back = lax.all_to_all(partial_out, "dev", split_axis=0, concat_axis=0, tiled=True)
    local_mix = jnp.einsum(
        "rec,ecd->rd", slot_gate, back.astype(jnp.float32), precision=lax.Precision.HIGHEST
    )
    combined = lax.psum(local_mix, "side")
    return (context, combined.astype(jnp.bfloat16))


def solution(mesh):
    in_specs = (
        P("dev", "side"),
        P("dev", None, "side"),
        P("dev", None, "side"),
        P("dev", "side"),
        P("dev", "side"),
        P("dev"),
        P("dev", None),
        P(),
        P("dev", None),
        P("dev", None),
        P("dev", None, "side"),
        P("dev", None, "side"),
        P("dev", "side", None),
    )
    out_specs = (P("dev", "side"), P("dev", None))
    return jax.shard_map(
        per_device, mesh=mesh, in_specs=in_specs, out_specs=out_specs, check_vma=False
    )
```

profile of v0, /device:TPU:2, one launch (start us, length us, event | category | flops | bytes accessed | tf_op | source)
XLA Modules:
  0.0 173.4 jit_solution(5468898151774488935)
XLA Ops:
  0.6 0.8 copy.38
  1.7 0.6 reduce-window.6
  2.3 0.2 slice_reduce_fusion
  2.9 0.7 reduce_sum.56
  3.6 0.7 broadcast_divide_fusion
  4.3 0.7 multiply_reduce_fusion
  5.2 0.7 convert_element_type.92
  5.9 1.1 fusion.32
  7.0 2.4 %convolution_convert_fusion = bf16[64,8,4096]{2,1,0:T(8,128)(2,1)S(1)} fusion(bf16[32,64,8]{0,2,1:T(8,128)(2,1)S(1)} %copy.43, bf16[32,4096]{1,0:T(8,128)(2,1)} %param.19, f32[4096]{0:T(1024)S(1)} %convert_element_type.92, f32[32]{0:T(128)S(1)} %add_rsqrt_fusion), kind=kOutput, calls=%fused_computation.7 | convolution fusion | flops 136839168 | bytes 4505728 | tf_op jit(solution)/shard_map/rec,rd->ecd/dot_general | solution.py:87
  9.5 61.6 %all_to_all.10 = bf16[64,8,4096]{2,1,0:T(8,128)(2,1)S(1)} all-to-all(bf16[64,8,4096]{2,1,0:T(8,128)(2,1)S(1)} %convolution_convert_fusion), channel_id=1, replica_groups=mesh['side'=2,'dev'=64] {'dev'}, dimensions={0} | all-to-all | bytes 8388608 | tf_op jit(solution)/shard_map/all_to_all | solution.py:90
  71.1 3.5 %fusion.4 = f32[64,8,768]{2,1,0:T(8,128)S(1)} fusion(bf16[64,8,4096]{2,1,0:T(8,128)(2,1)S(1)} %all_to_all.10, bf16[1,4096,768]{2,1,0:T(8,128)(2,1)S(1)} %bitcast.90), kind=kOutput, calls=%fused_computation.4 | convolution fusion | flops 3221225472 | bytes 12058624 | tf_op jit(solution)/shard_map/scd,df->scf/dot_general | solution.py:91
  74.6 3.6 %multiply_convert_fusion = bf16[64,8,768]{2,1,0:T(8,128)(2,1)S(1)} fusion(f32[64,8,768]{2,1,0:T(8,128)S(1)} %fusion.4, bf16[64,8,4096]{2,1,0:T(8,128)(2,1)S(1)} %all_to_all.10, bf16[1,4096,768]{2,1,0:T(8,128)(2,1)S(1)} %bitcast.92), kind=kOutput, calls=%fused_computation.15 | convolution fusion | flops 3223584768 | bytes 12845056 | tf_op jit(solution)/shard_map/scd,df->scf/dot_general | solution.py:92
  78.2 3.7 %fusion.6 = bf16[64,8,4096]{2,0,1:T(8,128)(2,1)S(1)} fusion(bf16[1,768,4096]{2,1,0:T(8,128)(2,1)S(1)} %bitcast.94, bf16[64,8,768]{2,1,0:T(8,128)(2,1)S(1)} %multiply_convert_fusion), kind=kOutput, calls=%fused_computation.6 | convolution fusion | flops 3223322624 | bytes 11272192 | tf_op jit(solution)/shard_map/scf,fd->scd/dot_general | solution.py:94
  81.9 4.3 %copy.45 = bf16[64,8,4096]{2,1,0:T(8,128)(2,1)} copy(bf16[64,8,4096]{2,0,1:T(8,128)(2,1)S(1)} %fusion.6) | data formatting | bytes 8388608 | tf_op jit(solution)/shard_map/convert_element_type | solution.py:96
  86.2 5.7 %all-to-all-start.1 = ((bf16[64,8,4096]{2,1,0:T(8,128)(2,1)}), bf16[64,8,4096]{2,1,0:T(8,128)(2,1)}, u32[]{:S(2)}, u32[]{:S(2)}) async-start(bf16[64,8,4096]{2,1,0:T(8,128)(2,1)} %copy.45), calls=%async_computation.1 | async-start | bytes 8388608 | tf_op jit(solution)/shard_map/all_to_all | solution.py:97
  92.1 0.2 fusion.49
  92.3 3.7 %fusion.48 = (f32[32,2,16]{2,1,0:T(2,128)S(1)}, f32[32,2,16,256]{3,2,1,0:T(8,128)S(1)}) fusion(bf16[32,2,16,128]{3,2,1,0:T(8,128)(2,1)S(1)} %bitcast.83, pred[32,256]{1,0:T(8,128)(4,1)S(1)} %iota_compare_fusion.4, bf16[32,256,256]{2,1,0:T(8,128)(2,1)} %param.14), kind=kOutput, calls=%fused_computation.59 | convolution fusion | flops 67894272 | bytes 5517312 | tf_op jit(solution)/shard_map/tgqd,tlgd->tgql/dot_general | solution.py:35
  96.0 0.4 fusion.30
  96.6 1.0 fusion.26
  97.6 0.8 copy.80
  98.4 0.2 copy.50
  98.6 47.8 %all-to-all-done.1 = bf16[64,8,4096]{2,1,0:T(8,128)(2,1)} async-done(((bf16[64,8,4096]{2,1,0:T(8,128)(2,1)}), bf16[64,8,4096]{2,1,0:T(8,128)(2,1)}, u32[]{:S(2)}, u32[]{:S(2)}) %all-to-all-start.1) | async-done | bytes 4194336 | tf_op jit(solution)/shard_map/all_to_all | solution.py:97
  146.4 4.4 %convolution_bitcast_fusion = f32[32,4096]{1,0:T(8,128)S(1)} fusion(f32[32,64,8]{0,2,1:T(8,128)S(1)} %copy.50, bf16[64,8,4096]{2,1,0:T(8,128)(2,1)} %all-to-all-done.1), kind=kOutput, calls=%fused_computation.8 | convolution fusion | flops 805306368 | bytes 4784128 | tf_op jit(solution)/shard_map/rec,ecd->rd/dot_general | solution.py:98
  150.8 22.6 %all-reduce.1 = bf16[32,4096]{1,0:T(8,128)(2,1)} all-reduce(f32[32,4096]{1,0:T(8,128)S(1)} %convolution_bitcast_fusion), channel_id=1, replica_groups=mesh['side'=2,'dev'=64] {'side'}, use_global_device_ids=true, to_apply=%region_9.10 | all-reduce | flops 131072 | bytes 786432 | tf_op jit(solution)/shard_map/psum | solution.py:101
  (43 shorter events, 1.2 us)
Async XLA Ops:
  7.0 64.1 %slice-start = ((s8[6291456]{0:T(1024)(128)(4,1)}), s8[4194304]{0:T(1024)(128)(4,1)S(1)}, s32[]{:S(2)}) async-start(s8[6291456]{0:T(1024)(128)(4,1)} %bitcast.89), calls=%async_computation.2 | async-start | bytes 8388608
  9.4 61.7 %slice-start.1 = ((s8[6291456]{0:T(1024)(128)(4,1)}), s8[2097152]{0:T(1024)(128)(4,1)S(1)}, s32[]{:S(2)}) async-start(s8[6291456]{0:T(1024)(128)(4,1)} %bitcast.89), calls=%async_computation.3 | async-start | bytes 4194304
  9.4 65.1 %slice-start.2 = ((s8[6291456]{0:T(1024)(128)(4,1)}), s8[4194304]{0:T(1024)(128)(4,1)S(1)}, s32[]{:S(2)}) async-start(s8[6291456]{0:T(1024)(128)(4,1)} %bitcast.91), calls=%async_computation.4 | async-start | bytes 8388608
  71.1 3.5 %slice-start.3 = ((s8[6291456]{0:T(1024)(128)(4,1)}), s8[2097152]{0:T(1024)(128)(4,1)S(1)}, s32[]{:S(2)}) async-start(s8[6291456]{0:T(1024)(128)(4,1)} %bitcast.91), calls=%async_computation.5 | async-start | bytes 4194304
  71.1 7.1 %slice-start.4 = ((s8[6291456]{0:T(1024)(128)(4,1)}), s8[4194304]{0:T(1024)(128)(4,1)S(1)}, s32[]{:S(2)}) async-start(s8[6291456]{0:T(1024)(128)(4,1)} %bitcast.93), calls=%async_computation.6 | async-start | bytes 8388608
  74.6 3.6 %slice-start.5 = ((s8[6291456]{0:T(1024)(128)(4,1)}), s8[2097152]{0:T(1024)(128)(4,1)S(1)}, s32[]{:S(2)}) async-start(s8[6291456]{0:T(1024)(128)(4,1)} %bitcast.93), calls=%async_computation.7 | async-start | bytes 4194304
  86.2 5.7 %copy-start = (bf16[32,4096]{1,0:T(8,128)(2,1)S(1)}, bf16[32,4096]{1,0:T(8,128)(2,1)}, u32[]{:S(2)}) copy-start(bf16[32,4096]{1,0:T(8,128)(2,1)} %param.13) | copy-start | bytes 786436
  86.2 5.8 %copy-start.1 = (bf16[32,256]{1,0:T(8,128)(2,1)S(1)}, bf16[32,256]{1,0:T(8,128)(2,1)}, u32[]{:S(2)}) copy-start(bf16[32,256]{1,0:T(8,128)(2,1)} %param.16) | copy-start | bytes 49156
  86.2 5.8 %copy-start.2 = (bf16[32,256]{1,0:T(8,128)(2,1)S(1)}, bf16[32,256]{1,0:T(8,128)(2,1)}, u32[]{:S(2)}) copy-start(bf16[32,256]{1,0:T(8,128)(2,1)} %param.17) | copy-start | bytes 49156
  86.2 5.8 %copy-start.3 = (s32[32]{0:T(128)S(1)}, s32[32]{0:T(128)}, u32[]{:S(2)}) copy-start(s32[32]{0:T(128)} %param.18) | copy-start | bytes 388
  86.2 60.2 %all-to-all-start.1 = ((bf16[64,8,4096]{2,1,0:T(8,128)(2,1)}), bf16[64,8,4096]{2,1,0:T(8,128)(2,1)}, u32[]{:S(2)}, u32[]{:S(2)}) async-start(bf16[64,8,4096]{2,1,0:T(8,128)(2,1)} %copy.45), calls=%async_computation.1 | async-start | bytes 8388608 | tf_op jit(solution)/shard_map/all_to_all | solution.py:97
  92.0 4.6 %copy-start.4 = (bf16[32,256,256]{2,1,0:T(8,128)(2,1)S(1)}, bf16[32,256,256]{2,1,0:T(8,128)(2,1)}, u32[]{:S(2)}) copy-start(bf16[32,256,256]{2,1,0:T(8,128)(2,1)} %param.15) | copy-start | bytes 12582916
where the time goes:
time: 174 us; the launch traced here: 173 us
  blocking collectives  84.2 us (48%)
  waiting for transfers between devices  47.8 us (27%)
  matrix products  22.4 us (13%)
  local copies, waits for them, and re-layouts  6.81 us (4%)
  starting transfers between devices  5.68 us (3%)
  other arithmetic  5.51 us (3%)
    all_to_all x1, blocking collectives, per_device(): lax.all_to_all(buffer, 'dev', split_axis=0, concat_axis=0, tiled=True)  61.6 us
    all_to_all x1, waiting for transfers between devices, per_device(): lax.all_to_all(partial_out, 'dev', split_axis=0, concat_axis=0, tiled=True)  47.8 us
    psum x1, blocking collectives, per_device(): combined = lax.psum(local_mix, 'side')  22.6 us
    all_to_all x1, starting transfers between devices, per_device(): lax.all_to_all(partial_out, 'dev', split_axis=0, concat_axis=0, tiled=True)  5.68 us
    dot_general x1, matrix products, per_device(): jnp.einsum('rec,ecd->rd', slot_gate, back.astype(jnp.float32), precision=...  4.42 us
    convert_element_type x1, local copies, waits for them, and re-layouts, per_device(): partial_out = jnp.einsum('scf,fd->scd', activation, w_down[0], preferred_...  4.27 us
    dot_general x1, matrix products, attend_local(): jnp.einsum('tgqd,tlgd->tgql', query_heads, key_heads, preferred_element_t...  3.67 us
    dot_general x1, matrix products, per_device(): jnp.einsum('scf,fd->scd', activation, w_down[0], preferred_element_type=j...  3.66 us
  transfers between devices with their start and end apart: 1, of which 1 were waited for; matrix products, arithmetic and copies ran while one was open for 4% of the time, Pallas kernels for 0%

commit v1 on v0

--- a/solution.py
+++ b/solution.py
@@ -98,7 +98,8 @@
     local_mix = jnp.einsum(
         "rec,ecd->rd", slot_gate, back.astype(jnp.float32), precision=lax.Precision.HIGHEST
     )
-    combined = lax.psum(local_mix, "side")
+    terms = lax.all_gather(local_mix, "side", axis=0, tiled=False)
+    combined = terms.sum(axis=0)
     return (context, combined.astype(jnp.bfloat16))
 
 

time: 174 us -> 193 us (1.11)
  waiting for transfers between devices: 47.8 us -> 70.7 us
  blocking collectives: 84.2 us -> 61.6 us
  between operations: 0.93 us -> 14.3 us
  matrix products: 22.4 us -> 25 us
  other arithmetic: 5.51 us -> 7.59 us
    psum x1 -> x0, blocking collectives: 22.6 us -> none  [per_device(): combined = lax.psum(local_mix, 'side')]
    all_gather x0 -> x1, waiting for transfers between devices: none -> 20.6 us  [per_device(): terms = lax.all_gather(local_mix, 'side', axis=0, tiled=False)]
    all_to_all x1, waiting for transfers between devices: 47.8 us -> 50.1 us  [per_device(): lax.all_to_all(partial_out, 'dev', split_axis=0, concat_axis=0, tiled=True)]
    reduce_sum x0 -> x1, other arithmetic: none -> 2.07 us  [per_device(): combined = terms.sum(axis=0)]
    dot_general x1, matrix products: 1 us -> 2.96 us  [attend_local(): jnp.einsum('tgql,tlgd->tgqd', attn_weights, value_heads, preferred_elemen...]
  transfers between devices with their start and end apart: 1 -> 2, of which waited for: 1 -> 2; matrix products, arithmetic and copies ran while one was open for 4% -> 4% of each run, Pallas kernels for 0% -> 0%
where the time goes in v1:
time: 193 us; the launch traced here: 192 us
  waiting for transfers between devices  70.7 us (37%)
  blocking collectives  61.6 us (32%)
  matrix products  25 us (13%)
  between operations  14.3 us (7%)
  other arithmetic  7.59 us (4%)
  local copies, waits for them, and re-layouts  6.81 us (4%)
  starting transfers between devices  5.93 us (3%)
    all_to_all x1, blocking collectives, per_device(): lax.all_to_all(buffer, 'dev', split_axis=0, concat_axis=0, tiled=True)  61.6 us
    all_to_all x1, waiting for transfers between devices, per_device(): lax.all_to_all(partial_out, 'dev', split_axis=0, concat_axis=0, tiled=True)  50.1 us
    all_gather x1, waiting for transfers between devices, per_device(): terms = lax.all_gather(local_mix, 'side', axis=0, tiled=False)  20.6 us
    all_to_all x1, starting transfers between devices, per_device(): lax.all_to_all(partial_out, 'dev', split_axis=0, concat_axis=0, tiled=True)  5.67 us
    dot_general x1, matrix products, per_device(): jnp.einsum('rec,ecd->rd', slot_gate, back.astype(jnp.float32), precision=...  5.22 us
    convert_element_type x1, local copies, waits for them, and re-layouts, per_device(): partial_out = jnp.einsum('scf,fd->scd', activation, w_down[0], preferred_...  4.27 us
  transfers between devices with their start and end apart: 2, of which 2 were waited for; matrix products, arithmetic and copies ran while one was open for 4% of the time, Pallas kernels for 0%

profile of v1, /device:TPU:2, one launch (start us, length us, event | category | flops | bytes accessed | tf_op | source)
XLA Modules:
  0.0 192.0 jit_solution(13323553420732560574)
XLA Ops:
  7.2 0.8 copy.38
  8.2 0.6 reduce-window.6
  9.4 0.7 reduce_sum.65
  10.1 0.7 broadcast_divide_fusion
  10.9 0.7 multiply_reduce_fusion
  11.7 0.7 convert_element_type.92
  12.4 1.1 fusion.32
  13.6 2.4 %convolution_convert_fusion = bf16[64,8,4096]{2,1,0:T(8,128)(2,1)S(1)} fusion(bf16[32,64,8]{0,2,1:T(8,128)(2,1)S(1)} %copy.43, bf16[32,4096]{1,0:T(8,128)(2,1)} %param.19, f32[4096]{0:T(1024)S(1)} %convert_element_type.92, f32[32]{0:T(128)S(1)} %add_rsqrt_fusion), kind=kOutput, calls=%fused_computation.7 | convolution fusion | flops 136839168 | bytes 4505728 | tf_op jit(solution)/shard_map/rec,rd->ecd/dot_general | solution.py:87
  16.0 61.6 %all_to_all.10 = bf16[64,8,4096]{2,1,0:T(8,128)(2,1)S(1)} all-to-all(bf16[64,8,4096]{2,1,0:T(8,128)(2,1)S(1)} %convolution_convert_fusion), channel_id=1, replica_groups=mesh['side'=2,'dev'=64] {'dev'}, dimensions={0} | all-to-all | bytes 8388608 | tf_op jit(solution)/shard_map/all_to_all | solution.py:90
  77.7 3.4 %fusion.4 = f32[64,8,768]{2,1,0:T(8,128)S(1)} fusion(bf16[64,8,4096]{2,1,0:T(8,128)(2,1)S(1)} %all_to_all.10, bf16[1,4096,768]{2,1,0:T(8,128)(2,1)S(1)} %bitcast.92), kind=kOutput, calls=%fused_computation.4 | convolution fusion | flops 3221225472 | bytes 12058624 | tf_op jit(solution)/shard_map/scd,df->scf/dot_general | solution.py:91
  81.2 3.5 %multiply_convert_fusion = bf16[64,8,768]{2,1,0:T(8,128)(2,1)S(1)} fusion(f32[64,8,768]{2,1,0:T(8,128)S(1)} %fusion.4, bf16[64,8,4096]{2,1,0:T(8,128)(2,1)S(1)} %all_to_all.10, bf16[1,4096,768]{2,1,0:T(8,128)(2,1)S(1)} %bitcast.94), kind=kOutput, calls=%fused_computation.15 | convolution fusion | flops 3223584768 | bytes 12845056 | tf_op jit(solution)/shard_map/scd,df->scf/dot_general | solution.py:92
  84.7 3.7 %fusion.6 = bf16[64,8,4096]{2,0,1:T(8,128)(2,1)S(1)} fusion(bf16[1,768,4096]{2,1,0:T(8,128)(2,1)S(1)} %bitcast.96, bf16[64,8,768]{2,1,0:T(8,128)(2,1)S(1)} %multiply_convert_fusion), kind=kOutput, calls=%fused_computation.6 | convolution fusion | flops 3223322624 | bytes 11272192 | tf_op jit(solution)/shard_map/scf,fd->scd/dot_general | solution.py:94
  88.4 4.3 %copy.45 = bf16[64,8,4096]{2,1,0:T(8,128)(2,1)} copy(bf16[64,8,4096]{2,0,1:T(8,128)(2,1)S(1)} %fusion.6) | data formatting | bytes 8388608 | tf_op jit(solution)/shard_map/convert_element_type | solution.py:96
  92.7 5.7 %all-to-all-start.1 = ((bf16[64,8,4096]{2,1,0:T(8,128)(2,1)}), bf16[64,8,4096]{2,1,0:T(8,128)(2,1)}, u32[]{:S(2)}, u32[]{:S(2)}) async-start(bf16[64,8,4096]{2,1,0:T(8,128)(2,1)} %copy.45), calls=%async_computation.1 | async-start | bytes 8388608 | tf_op jit(solution)/shard_map/all_to_all | solution.py:97
  98.4 0.3 all-gather.3.cloned.1.call-start
  99.0 0.2 fusion.49
  99.2 3.5 %fusion.48 = (f32[32,2,16]{2,1,0:T(2,128)S(1)}, f32[32,2,16,256]{3,2,1,0:T(8,128)S(1)}) fusion(bf16[32,2,16,128]{3,2,1,0:T(8,128)(2,1)S(1)} %bitcast.85, pred[32,256]{1,0:T(8,128)(4,1)S(1)} %iota_compare_fusion.4, bf16[32,256,256]{2,1,0:T(8,128)(2,1)} %param.14), kind=kOutput, calls=%fused_computation.59 | convolution fusion | flops 67894272 | bytes 5517312 | tf_op jit(solution)/shard_map/tgqd,tlgd->tgql/dot_general | solution.py:35
  102.8 50.1 %all-to-all-done.1 = bf16[64,8,4096]{2,1,0:T(8,128)(2,1)} async-done(((bf16[64,8,4096]{2,1,0:T(8,128)(2,1)}), bf16[64,8,4096]{2,1,0:T(8,128)(2,1)}, u32[]{:S(2)}, u32[]{:S(2)}) %all-to-all-start.1) | async-done | bytes 4194336 | tf_op jit(solution)/shard_map/all_to_all | solution.py:97
  152.9 5.2 %convolution_bitcast_fusion = f32[32,4096]{1,0:T(8,128)} fusion(f32[32,64,8]{0,2,1:T(8,128)S(1)} %copy.50, bf16[64,8,4096]{2,1,0:T(8,128)(2,1)} %all-to-all-done.1), kind=kOutput, calls=%fused_computation.8 | convolution fusion | flops 805306368 | bytes 4784128 | tf_op jit(solution)/shard_map/rec,ecd->rd/dot_general | solution.py:98
  158.2 0.4 fusion.30
  158.7 3.0 %fusion.26 = bf16[32,2,16,128]{3,2,1,0:T(8,128)(2,1)S(1)} fusion(f32[32,2,16,256]{3,2,1,0:T(8,128)S(1)} %get-tuple-element.7, f32[32,2,16]{2,1,0:T(2,128)S(1)} %get-tuple-element.5, f32[32,2,16]{2,1,0:T(2,128)S(1)} %multiply_maximum_fusion, f32[32,2,128]{2,1,0:T(2,128)S(1)} %reshape.127, f32[32,2,16]{2,1,0:T(2,128)S(1)} %get-tuple-element.4, ...), kind=kOutput, calls=%fused_computation.21 | convolution fusion | flops 68288512 | bytes 5550080 | tf_op jit(solution)/shard_map/tgql,tlgd->tgqd/dot_general | solution.py:51
  161.6 0.8 copy.80
  162.5 20.6 %all-gather.3.cloned.1.call-done = f32[64,4096]{1,0:T(8,128)} async-done(((f32[32,4096]{1,0:T(8,128)}), f32[64,4096]{1,0:T(8,128)}) %all-gather.3.cloned.1.call-update) | async-done | bytes 1048592 | tf_op jit(solution)/shard_map/all_gather | solution.py:101
  183.0 2.1 %reduce_sum.69 = bf16[32,4096]{1,0:T(8,128)(2,1)} reduce(f32[2,32,4096]{2,1,0:T(8,128)} %bitcast.83, f32[]{:T(128)} %constant.6.clone.1), dimensions={0}, to_apply=%region_9.10 | reduce | flops 131072 | bytes 1310724 | tf_op jit(solution)/shard_map/reduce_sum | solution.py:102
  (44 shorter events, 1.5 us)
Async XLA Ops:
  13.6 64.1 %slice-start = ((s8[6291456]{0:T(1024)(128)(4,1)}), s8[4194304]{0:T(1024)(128)(4,1)S(1)}, s32[]{:S(2)}) async-start(s8[6291456]{0:T(1024)(128)(4,1)} %bitcast.91), calls=%async_computation.3 | async-start | bytes 8388608
  16.0 61.7 %slice-start.1 = ((s8[6291456]{0:T(1024)(128)(4,1)}), s8[2097152]{0:T(1024)(128)(4,1)S(1)}, s32[]{:S(2)}) async-start(s8[6291456]{0:T(1024)(128)(4,1)} %bitcast.91), calls=%async_computation.4 | async-start | bytes 4194304
  16.0 65.1 %slice-start.2 = ((s8[6291456]{0:T(1024)(128)(4,1)}), s8[4194304]{0:T(1024)(128)(4,1)S(1)}, s32[]{:S(2)}) async-start(s8[6291456]{0:T(1024)(128)(4,1)} %bitcast.93), calls=%async_computation.5 | async-start | bytes 8388608
  77.6 3.5 %slice-start.3 = ((s8[6291456]{0:T(1024)(128)(4,1)}), s8[2097152]{0:T(1024)(128)(4,1)S(1)}, s32[]{:S(2)}) async-start(s8[6291456]{0:T(1024)(128)(4,1)} %bitcast.93), calls=%async_computation.6 | async-start | bytes 4194304
  77.6 7.1 %slice-start.4 = ((s8[6291456]{0:T(1024)(128)(4,1)}), s8[4194304]{0:T(1024)(128)(4,1)S(1)}, s32[]{:S(2)}) async-start(s8[6291456]{0:T(1024)(128)(4,1)} %bitcast.95), calls=%async_computation.7 | async-start | bytes 8388608
  81.1 3.6 %slice-start.5 = ((s8[6291456]{0:T(1024)(128)(4,1)}), s8[2097152]{0:T(1024)(128)(4,1)S(1)}, s32[]{:S(2)}) async-start(s8[6291456]{0:T(1024)(128)(4,1)} %bitcast.95), calls=%async_computation.8 | async-start | bytes 4194304
  92.7 6.0 %copy-start = (bf16[32,4096]{1,0:T(8,128)(2,1)S(1)}, bf16[32,4096]{1,0:T(8,128)(2,1)}, u32[]{:S(2)}) copy-start(bf16[32,4096]{1,0:T(8,128)(2,1)} %param.13) | copy-start | bytes 786436
  92.7 6.0 %copy-start.1 = (bf16[32,256]{1,0:T(8,128)(2,1)S(1)}, bf16[32,256]{1,0:T(8,128)(2,1)}, u32[]{:S(2)}) copy-start(bf16[32,256]{1,0:T(8,128)(2,1)} %param.16) | copy-start | bytes 49156
  92.7 6.0 %copy-start.2 = (bf16[32,256]{1,0:T(8,128)(2,1)S(1)}, bf16[32,256]{1,0:T(8,128)(2,1)}, u32[]{:S(2)}) copy-start(bf16[32,256]{1,0:T(8,128)(2,1)} %param.17) | copy-start | bytes 49156
  92.7 6.2 %copy-start.3 = (s32[32]{0:T(128)S(1)}, s32[32]{0:T(128)}, u32[]{:S(2)}) copy-start(s32[32]{0:T(128)} %param.18) | copy-start | bytes 388
  92.7 60.2 %all-to-all-start.1 = ((bf16[64,8,4096]{2,1,0:T(8,128)(2,1)}), bf16[64,8,4096]{2,1,0:T(8,128)(2,1)}, u32[]{:S(2)}, u32[]{:S(2)}) async-start(bf16[64,8,4096]{2,1,0:T(8,128)(2,1)} %copy.45), calls=%async_computation.1 | async-start | bytes 8388608 | tf_op jit(solution)/shard_map/all_to_all | solution.py:97
  98.4 84.7 %all-gather.3.cloned.1.call-start = ((), (), s32[]{:S(2)}) async-start(), calls=%async_computation.2 | async-start | bytes 1572864 | tf_op jit(solution)/shard_map/all_gather | solution.py:101
Sparse Core Ops, SparseCore 0:
  158.2 24.7 all-gather.2
